TPU v7x, 32 devices: a whole 2x2x4 slice. The times are simulated.
32 devices in a mesh: tm: 8 (over y, x, core), stream: 4 (over z).
Axes of the slice: x: 2, y: 2, z: 4, core: 2. Of those that a mesh axis runs over, the one named last changes fastest.
Arguments:
- tokens: bfloat16 [4096, 2048], P(('tm', 'stream')), may hold values from -6 to 6
- w_query: bfloat16 [2048, 2048], P('stream'), may hold values from -0.125 to 0.125
- w_key: bfloat16 [2048, 2048], P('stream'), may hold values from -0.125 to 0.125
- w_value: bfloat16 [2048, 2048], P('stream'), may hold values from -0.125 to 0.125
- decay_proj: bfloat16 [2048, 16], P('stream'), may hold values from -0.125 to 0.125
- beta_proj: bfloat16 [2048, 16], P('stream'), may hold values from -0.125 to 0.125
- decay_rate: float32 [16], replicated, may hold values from 0.00024414062 to 0.1
- beta_bias: float32 [16], replicated, may hold values from -7 to 0
- norm_gain: float32 [128], replicated, may hold values from 0.5 to 1.5
Outputs:
- mixed: bfloat16 [4096, 2048], P(('tm', 'stream'))
All inputs are finite; a program needn't handle non-finite values.
Results may differ from a plain program's by a relative error of at most 0.0073.
Values may be sent and summed in bfloat16 or wider, within the bound.
A program may use at most 128 MiB of HBM per device.

v0:
```python
import jax
import jax.numpy as jnp
from jax import lax
from jax.sharding import PartitionSpec as P

HEADS = 16
DK = 128
DV = 128
GROUP = 256


highest_precision = lax.Precision.HIGHEST


def carried_in(part, axis, combine, identity):
    place = lax.axis_index(axis)
    gathered = jax.tree.map(lambda a: lax.all_gather(a, axis), part)
    state = jax.tree.map(lambda a, e: jnp.zeros_like(a) + jnp.asarray(e, a.dtype), part, identity)

    def one(lap, state):
        return combine(
            state, jax.tree.map(lambda a: lax.dynamic_index_in_dim(a, lap, 0, False), gathered)
        )

    return lax.fori_loop(0, place, one, state)


def add_rows(inputs, piece):
    return jnp.dot(inputs, piece, preferred_element_type=jnp.float32)


def compose_pairs(earlier, later):
    first_map, first_shift = earlier
    second_map, second_shift = later
    joined_map = jnp.einsum("udf,ufe->ude", first_map, second_map, precision=highest_precision)
    joined_shift = (
        jnp.einsum("ued,udf->uef", first_shift, second_map, precision=highest_precision)
        + second_shift
    )
    return (joined_map, joined_shift)


def shards(
    tokens, w_query, w_key, w_value, decay_proj, beta_proj, decay_rate, beta_bias, norm_gain
):
    local_rows = tokens.shape[0]
    streams = lax.axis_size("stream")
    per_device = HEADS // streams

    def fold_one(piece):
        return add_rows(tokens, piece)

    raw_query = fold_one(lax.all_gather(w_query, "stream", axis=0, tiled=True))
    raw_key = fold_one(lax.all_gather(w_key, "stream", axis=0, tiled=True))
    raw_value = fold_one(lax.all_gather(w_value, "stream", axis=0, tiled=True))
    pieces = (
        lax.all_gather(decay_proj, "stream", axis=0, tiled=True),
        lax.all_gather(beta_proj, "stream", axis=0, tiled=True),
    )
    decay_logit, beta_logit = tuple((add_rows(tokens, piece) for piece in pieces))
    query_heads = raw_query.reshape(local_rows, HEADS, DK)
    key_heads = raw_key.reshape(local_rows, HEADS, DK)
    queries = (
        (
            query_heads
            * lax.rsqrt(jnp.sum(query_heads * query_heads, -1, keepdims=True) + 1e-06)
            * DK ** (-0.5)
        )
        .astype(jnp.bfloat16)
        .reshape(local_rows, HEADS * DK)
    )
    key_rows = (
        (key_heads * lax.rsqrt(jnp.sum(key_heads * key_heads, -1, keepdims=True) + 1e-06))
        .astype(jnp.bfloat16)
        .reshape(local_rows, HEADS * DK)
    )
    values = raw_value.astype(jnp.bfloat16)
    log_decay = (-decay_rate * jax.nn.softplus(decay_logit)).astype(jnp.bfloat16)
    strength = jax.nn.sigmoid(beta_logit + beta_bias).astype(jnp.bfloat16)
    got_query, got_key, got_value, got_decay, got_strength = (
        lax.all_to_all(queries, "stream", split_axis=1, concat_axis=0, tiled=True),
        lax.all_to_all(key_rows, "stream", split_axis=1, concat_axis=0, tiled=True),
        lax.all_to_all(values, "stream", split_axis=1, concat_axis=0, tiled=True),
        lax.all_to_all(log_decay, "stream", split_axis=1, concat_axis=0, tiled=True),
        lax.all_to_all(strength, "stream", split_axis=1, concat_axis=0, tiled=True),
    )
    block_rows = got_query.shape[0]
    num_blocks = block_rows // GROUP
    query_b = (
        got_query.reshape(num_blocks, GROUP, per_device, DK)
        .astype(jnp.float32)
        .transpose(0, 2, 1, 3)
    )
    key_b = (
        got_key.reshape(num_blocks, GROUP, per_device, DK).astype(jnp.float32).transpose(0, 2, 1, 3)
    )
    value_b = (
        got_value.reshape(num_blocks, GROUP, per_device, DV)
        .astype(jnp.float32)
        .transpose(0, 2, 1, 3)
    )
    decay_b = (
        got_decay.reshape(num_blocks, GROUP, per_device).astype(jnp.float32).transpose(0, 2, 1)
    )
    strength_b = (
        got_strength.reshape(num_blocks, GROUP, per_device).astype(jnp.float32).transpose(0, 2, 1)
    )
    positions = jnp.arange(GROUP)
    strict = positions[:, None] > positions[None, :]
    inclusive_mask = positions[:, None] >= positions[None, :]
    identity = jnp.eye(GROUP, dtype=jnp.float32)
    key_identity = jnp.eye(DK, dtype=jnp.float32)
    cumulative = jnp.cumsum(decay_b, axis=2)
    growth = jnp.exp(cumulative)
    last_log = cumulative[..., -1:]
    tail = jnp.exp(last_log - cumulative)
    key_products = jnp.einsum("nucd,numd->nucm", key_b, key_b, precision=highest_precision)
    spread = cumulative[..., :, None] - cumulative[..., None, :]
    decay_matrix = jnp.exp(jnp.where(inclusive_mask, spread, 0.0))
    lower = (
        jnp.where(strict, strength_b[..., :, None] * decay_matrix * key_products, 0.0) + identity
    )
    right_side = jnp.concatenate(
        [(strength_b * growth)[..., None] * key_b, strength_b[..., None] * value_b], -1
    )
    solved = jax.scipy.linalg.solve_triangular(lower, right_side, lower=True, unit_diagonal=True)
    weights_w = solved[..., :DK]
    updates = solved[..., DK:]
    key_tail = tail[..., None] * key_b
    attention_scores = jnp.where(
        inclusive_mask,
        jnp.einsum("nucd,numd->nucm", query_b, key_b, precision=highest_precision) * decay_matrix,
        0.0,
    )
    query_grown = growth[..., None] * query_b
    block_map = jnp.exp(last_log)[..., None] * key_identity - jnp.einsum(
        "nucd,nuce->nude", weights_w, key_tail, precision=highest_precision
    )
    block_shift = jnp.einsum("nuce,nucd->nued", updates, key_tail, precision=highest_precision)

    def compose_step(carry, pair):
        return (compose_pairs(carry, pair), carry)

    start_map = jnp.broadcast_to(key_identity, (per_device, DK, DK))
    start_shift = jnp.zeros((per_device, DV, DK), jnp.float32)
    totals, prefixes = lax.scan(compose_step, (start_map, start_shift), (block_map, block_shift))
    total_map, total_shift = totals
    prefix_map, prefix_shift = prefixes
    scanned = carried_in((total_map, total_shift), "tm", compose_pairs, (start_map, start_shift))
    state_in = scanned[1]
    block_states = (
        jnp.einsum("ued,nudf->nuef", state_in, prefix_map, precision=highest_precision)
        + prefix_shift
    )
    fresh = updates - jnp.einsum(
        "nucd,nued->nuce", weights_w, block_states, precision=highest_precision
    )
    read = jnp.einsum(
        "nucd,nued->nuce", query_grown, block_states, precision=highest_precision
    ) + jnp.einsum("nucm,nume->nuce", attention_scores, fresh, precision=highest_precision)
    readout = read.transpose(0, 2, 1, 3).reshape(block_rows, per_device * DV).astype(jnp.bfloat16)
    returned = lax.all_to_all(readout, "stream", split_axis=0, concat_axis=1, tiled=True)
    head_read = returned.reshape(local_rows, HEADS, DV).astype(jnp.float32)
    normed = (
        head_read
        * lax.rsqrt(jnp.mean(head_read * head_read, -1, keepdims=True) + 1e-06)
        * norm_gain
    )
    return normed.reshape(local_rows, HEADS * DV).astype(jnp.bfloat16)


def solution(mesh):
    return jax.shard_map(
        shards,
        mesh=mesh,
        in_specs=(
            P(("tm", "stream"), None),
            P("stream", None),
            P("stream", None),
            P("stream", None),
            P("stream", None),
            P("stream", None),
            P(),
            P(),
            P(),
        ),
        out_specs=P(("tm", "stream"), None),
        check_vma=False,
    )
```

profile of v0, /device:TPU:6, one launch (start us, length us, event | category | flops | bytes accessed | tf_op | source)
XLA Modules:
  0.0 679.3 jit_solution(14903224761476927591)
XLA Ops:
  8.8 13.6 %all_gather.27 = bf16[2048,16]{0,1:T(8,128)(2,1)S(1)} all-gather(bf16[512,16]{0,1:T(8,128)(2,1)S(1)} %copy-done.10), channel_id=1, replica_groups=mesh['tm'=8,'stream'=4] {'stream'}, dimensions={0}, use_global_device_ids=true | all-gather | bytes 81920 | tf_op jit(solution)/shard_map/all_gather | solution.py:57
  23.2 4.6 all-to-all-start
  27.9 20.2 %all_gather.29 = bf16[2048,16]{0,1:T(8,128)(2,1)S(1)} all-gather(bf16[512,16]{0,1:T(8,128)(2,1)S(1)} %copy-done.11), channel_id=1, replica_groups=mesh['tm'=8,'stream'=4] {'stream'}, dimensions={0}, use_global_device_ids=true | all-gather | bytes 81920 | tf_op jit(solution)/shard_map/all_gather | solution.py:58
  51.2 3.2 all-to-all-start.2
  54.4 2.4 reduce-window.6
  57.2 103.7 %all-gather.10.cloned.1.call-done = bf16[2048,2048]{1,0:T(8,128)(2,1)} async-done(((bf16[512,2048]{1,0:T(8,128)(2,1)}), bf16[2048,2048]{1,0:T(8,128)(2,1)}) %all-gather.10.cloned.1.call-update) | async-done | bytes 8388624 | tf_op jit(solution)/shard_map/all_gather | solution.py:54
  160.9 4.6 fusion.88
  165.5 144.8 %all-gather.12.cloned.1.call-done = bf16[2048,2048]{1,0:T(8,128)(2,1)} async-done(((bf16[512,2048]{1,0:T(8,128)(2,1)}), bf16[2048,2048]{1,0:T(8,128)(2,1)}) %all-gather.12.cloned.1.call-update) | async-done | bytes 8388624 | tf_op jit(solution)/shard_map/all_gather | solution.py:55
  310.3 4.6 convolution_convert_fusion
  315.8 3.5 all-to-all-start.4
  321.8 29.3 %all-to-all-done.4 = bf16[128,4,512]{2,0,1:T(8,128)(2,1)S(1)} async-done(((bf16[128,4,512]{2,0,1:T(8,128)(2,1)}), bf16[128,4,512]{2,0,1:T(8,128)(2,1)S(1)}, u32[]{:S(2)}, u32[]{:S(2)}) %all-to-all-start.4) | async-done | bytes 524320 | tf_op jit(solution)/shard_map/all_to_all | solution.py:83
  351.1 3.5 all-to-all-start.3
  355.1 1.3 reshape.187
  356.4 26.8 %all-to-all-done.3 = bf16[128,4,512]{2,0,1:T(8,128)(2,1)S(1)} async-done(((bf16[128,4,512]{2,0,1:T(8,128)(2,1)}), bf16[128,4,512]{2,0,1:T(8,128)(2,1)S(1)}, u32[]{:S(2)}, u32[]{:S(2)}) %all-to-all-start.3) | async-done | bytes 524320 | tf_op jit(solution)/shard_map/all_to_all | solution.py:82
  383.4 2.3 select_add_fusion
  385.8 5.8 while.31
  386.6 2.2 bitcast_dynamic-update-slice_fusion.5
  389.4 2.2 bitcast_dynamic-update-slice_fusion.5
  391.6 158.7 %custom-call.4 = f32[2,4,2,128,128]{3,4,2,1,0:T(8,128)} custom-call(f32[2,4,2,128,128]{4,3,2,1,0:T(8,128)} %bitcast.209), custom_call_target="InvertDiagBlocksLowerTriangular" | custom-call | tf_op jit(solution)/shard_map/jit(_solve_triangular)/vmap(vmap())/triangular_solve | solution.py:126
  553.0 2.1 convolution_subtract_fusion.1
  556.1 3.0 fusion.24
  559.1 3.2 fusion.30
  562.3 7.6 %while.32 = (s32[]{:T(128)}, f32[4,128,128]{1,2,0:T(8,128)S(1)}, f32[4,128,128]{1,2,0:T(8,128)}, f32[2,4,128,128]{2,3,0,1:T(8,128)}, f32[2,4,128,128]{2,3,0,1:T(...) while((s32[]{:T(128)}, f32[4,128,128]{1,2,0:T(8,128)S(1)}, ...), condition=%wide.region_5.6_spmd.clone, body=%wide.region_4.5_spmd.clone.sunk | while | flops 201523200 | bytes 6030995 | solution.py:146
  564.2 1.3 fusion.122
  568.0 1.3 fusion.122
  571.1 1.8 copy.179
  572.9 4.6 fusion.87
  577.6 1.2 copy.224
  578.9 1.6 reduce_sum.27
  581.0 1.7 fusion.43
  583.6 4.1 all-to-all-start.1
  587.7 15.2 %all-to-all-done.1 = bf16[128,4,512]{2,0,1:T(8,128)(2,1)} async-done(((bf16[128,4,512]{2,0,1:T(8,128)(2,1)}), bf16[128,4,512]{2,0,1:T(8,128)(2,1)}, u32[]{:S(2)}, u32[]{:S(2)}) %all-to-all-start.1) | async-done | bytes 524320 | tf_op jit(solution)/shard_map/all_to_all | solution.py:81
  602.9 2.0 reshape.159
  604.9 2.8 fusion.57
  607.7 18.3 %all-gather.16.cloned.1.call-done = f32[32,128,128]{2,1,0:T(8,128)} async-done(((f32[4,128,128]{2,1,0:T(8,128)}), f32[32,128,128]{2,1,0:T(8,128)}) %all-gather.16.cloned.1.call-update) | async-done | bytes 2097168 | tf_op jit(solution)/shard_map/all_gather | solution.py:17
  626.0 16.3 %while.30 = (s32[]{:T(128)}, f32[4,128,128]{1,2,0:T(8,128)S(1)}, s32[]{:T(128)}, f32[8,4,128,128]{3,2,1,0:T(8,128)}, f32[8,4,128,128]{3,2,1,0:T(8,128)}, /*index=5*/s32[]{:T(128)}, s32[]{:T(128)}, s32[]{:T(128)}) while((s32[]{:T(128)}, f32[4,128,128]{1,2,0:T(8,128)S(1)}, s32[]{:T(128)}, f32[8,4,128,128]{3,2,1,0:T(8,128)}, ...), condition=%wide.region_7.8_spmd, body=%wide.region_6.7_spmd.sunk | while | flops 100728832 | bytes 2621575 | solution.py:25
  627.2 1.6 fusion.116
  629.9 1.6 fusion.116
  632.6 1.6 fusion.116
  635.3 1.6 fusion.116
  638.1 1.6 fusion.116
  640.8 1.6 fusion.116
  642.4 1.8 fusion.29
  644.2 1.1 convolution_subtract_fusion
  645.3 1.2 fusion.49
  646.9 2.5 fusion.26
  650.8 4.6 all-to-all-start.5
  655.4 14.9 %all-to-all-done.5 = bf16[4,128,512]{2,1,0:T(8,128)(2,1)S(1)} async-done(((bf16[4,128,512]{2,1,0:T(8,128)(2,1)}), bf16[4,128,512]{2,1,0:T(8,128)(2,1)S(1)}, u32[]{:S(2)}, u32[]{:S(2)}) %all-to-all-start.5) | async-done | bytes 524320 | tf_op jit(solution)/shard_map/all_to_all | solution.py:162
  (141 shorter events, 33.8 us)
Async XLA Ops:
  6.5 15.8 %copy-start = (bf16[128,2048]{1,0:T(8,128)(2,1)S(1)}, bf16[128,2048]{1,0:T(8,128)(2,1)}, u32[]{:S(2)}) copy-start(bf16[128,2048]{1,0:T(8,128)(2,1)} %param.13) | copy-start | bytes 1572868
  6.5 154.3 %all-gather.10.cloned.1.call-start = ((), (), s32[]{:S(2)}) async-start(), calls=%async_computation.7 | async-start | bytes 10485760 | tf_op jit(solution)/shard_map/all_gather | solution.py:54
  7.3 1.5 copy-start.14
  7.3 1.5 copy-start.10
  7.3 20.6 %copy-start.11 = (bf16[512,16]{0,1:T(8,128)(2,1)S(1)}, bf16[512,16]{0,1:T(8,128)(2,1)}, u32[]{:S(2)}) copy-start(bf16[512,16]{0,1:T(8,128)(2,1)} %param.18) | copy-start | bytes 49156
  7.3 303.0 %all-gather.12.cloned.1.call-start = ((), (), s32[]{:S(2)}) async-start(), calls=%async_computation.8 | async-start | bytes 10485760 | tf_op jit(solution)/shard_map/all_gather | solution.py:55
  8.0 42.1 %copy-start.13 = (f32[16]{0:T(128)S(1)}, f32[16]{0:T(128)}, u32[]{:S(2)}) copy-start(f32[16]{0:T(128)} %param.20) | copy-start | bytes 196
  8.0 564.8 %all-gather.8.cloned.1.call-start = ((), (), s32[]{:S(2)}) async-start(), calls=%async_computation.6 | async-start | bytes 10485760 | tf_op jit(solution)/shard_map/all_gather | solution.py:53
  23.2 27.9 %all-to-all-start = ((bf16[128,4,4]{0,2,1:T(4,128)(2,1)}), bf16[128,4,4]{0,2,1:T(4,128)(2,1)S(1)}, u32[]{:S(2)}, u32[]{:S(2)}) async-start(bf16[128,4,4]{0,2,1:T(4,128)(2,1)} %bitcast.3), calls=%async_computation | async-start | bytes 8192 | tf_op jit(solution)/shard_map/all_to_all | solution.py:84
  51.2 264.6 %all-to-all-start.2 = ((bf16[128,4,4]{0,2,1:T(4,128)(2,1)}), bf16[128,4,4]{0,2,1:T(4,128)(2,1)S(1)}, u32[]{:S(2)}, u32[]{:S(2)}) async-start(bf16[128,4,4]{0,2,1:T(4,128)(2,1)} %bitcast.11), calls=%async_computation.2 | async-start | bytes 8192 | tf_op jit(solution)/shard_map/all_to_all | solution.py:85
  315.8 35.3 %all-to-all-start.4 = ((bf16[128,4,512]{2,0,1:T(8,128)(2,1)}), bf16[128,4,512]{2,0,1:T(8,128)(2,1)S(1)}, u32[]{:S(2)}, u32[]{:S(2)}) async-start(bf16[128,4,512]{2,0,1:T(8,128)(2,1)} %bitcast.160), calls=%async_computation.4 | async-start | bytes 1048576 | tf_op jit(solution)/shard_map/all_to_all | solution.py:83
  351.1 32.2 %all-to-all-start.3 = ((bf16[128,4,512]{2,0,1:T(8,128)(2,1)}), bf16[128,4,512]{2,0,1:T(8,128)(2,1)S(1)}, u32[]{:S(2)}, u32[]{:S(2)}) async-start(bf16[128,4,512]{2,0,1:T(8,128)(2,1)} %bitcast.161), calls=%async_computation.3 | async-start | bytes 1048576 | tf_op jit(solution)/shard_map/all_to_all | solution.py:82
  354.6 253.1 %all-gather.14.cloned.1.call-start = ((), (), s32[]{:S(2)}) async-start(), calls=%async_computation.9 | async-start | bytes 2359296 | tf_op jit(solution)/shard_map/all_gather | solution.py:17
  383.4 172.7 %copy-start.1 = (bf16[2,256,4,128]{3,2,1,0:T(4,128)(2,1)}, bf16[2,256,4,128]{3,2,1,0:T(4,128)(2,1)S(1)}, u32[]{:S(2)}) copy-start(bf16[2,256,4,128]{3,2,1,0:T(4,128)(2,1)S(1)} %reshape.160) | copy-start | bytes 1572868
  391.6 158.7 %copy-start.6 = (f32[2,4,256,256]{3,2,1,0:T(8,128)}, f32[2,4,256,256]{3,2,1,0:T(8,128)S(1)}, u32[]{:S(2)}) copy-start(f32[2,4,256,256]{3,2,1,0:T(8,128)S(1)} %get-tuple-element.409) | copy-start | bytes 6291460
  550.3 1.2 copy-start.8
  550.3 1.6 copy-start.9
  562.3 1.9 copy-start.5
  566.1 1.9 copy-start.5
  570.8 55.2 %all-gather.16.cloned.1.call-start = ((), (), s32[]{:S(2)}) async-start(), calls=%async_computation.10 | async-start | bytes 2359296 | tf_op jit(solution)/shard_map/all_gather | solution.py:17
  577.5 1.4 copy-start.3
  582.7 22.1 %copy-start.2 = (bf16[2,256,4,128]{3,2,1,0:T(4,128)(2,1)S(1)}, bf16[2,256,4,128]{3,2,1,0:T(4,128)(2,1)}, u32[]{:S(2)}) copy-start(bf16[2,256,4,128]{3,2,1,0:T(4,128)(2,1)} %copy-done.1) | copy-start | bytes 1572868
  583.6 19.3 %all-to-all-start.1 = ((bf16[128,4,512]{2,0,1:T(8,128)(2,1)}), bf16[128,4,512]{2,0,1:T(8,128)(2,1)}, u32[]{:S(2)}, u32[]{:S(2)}) async-start(bf16[128,4,512]{2,0,1:T(8,128)(2,1)} %bitcast.200), calls=%async_computation.1 | async-start | bytes 1048576 | tf_op jit(solution)/shard_map/all_to_all | solution.py:81
  644.2 1.1 copy-start.7
  645.3 1.6 copy-start.4
  649.4 6.0 copy-start.12
  650.8 19.5 %all-to-all-start.5 = ((bf16[4,128,512]{2,1,0:T(8,128)(2,1)}), bf16[4,128,512]{2,1,0:T(8,128)(2,1)S(1)}, u32[]{:S(2)}, u32[]{:S(2)}) async-start(bf16[4,128,512]{2,1,0:T(8,128)(2,1)} %convert_element_type.98), calls=%async_computation.5 | async-start | bytes 1048576 | tf_op jit(solution)/shard_map/all_to_all | solution.py:162
Sparse Core Ops, SparseCore 0:
  8.9 151.9 all-gather.9
  162.4 147.8 all-gather.11
  311.9 169.0 all-gather.7
  570.9 25.4 all-gather.13
  598.2 27.7 all-gather.15
where the time goes:
time: 682 us; the launch traced here: 679 us
  waiting for transfers between devices  355 us (52%)
  other arithmetic  171 us (25%)
  matrix products  50.9 us (7%)
  blocking collectives  33.7 us (5%)
  local copies, waits for them, and re-layouts  30.6 us (4%)
  starting transfers between devices  24 us (4%)
  between operations  13.6 us (2%)
    another operation x5, other arithmetic, shards(): jax.scipy.linalg.solve_triangular(lower, right_side, lower=True, unit_dia...  160 us
    all_gather x1, waiting for transfers between devices, shards(): raw_value = fold_one(lax.all_gather(w_value, 'stream', axis=0, tiled=True))  145 us
    all_gather x1, waiting for transfers between devices, shards(): raw_key = fold_one(lax.all_gather(w_key, 'stream', axis=0, tiled=True))  104 us
    all_to_all x1, waiting for transfers between devices, shards(): lax.all_to_all(values, 'stream', split_axis=1, concat_axis=0, tiled=True)  29.3 us
    all_to_all x1, waiting for transfers between devices, shards(): lax.all_to_all(key_rows, 'stream', split_axis=1, concat_axis=0, tiled=True)  26.8 us
    all_gather x1, blocking collectives, shards(): lax.all_gather(beta_proj, 'stream', axis=0, tiled=True)  20.2 us
    all_gather x2, waiting for transfers between devices, carried_in(): gathered = jax.tree.map(lambda a: lax.all_gather(a, axis), part)  18.3 us
    dot_general x5, matrix products, add_rows(): return jnp.dot(inputs, piece, preferred_element_type=jnp.float32)  15.6 us
  transfers between devices with their start and end apart: 11, of which 7 were waited for; matrix products, arithmetic and copies ran while one was open for 33% of the time, Pallas kernels for 0%

commit v1 on v0

v1 whole, which is shorter than its diff:
```python
import functools

import jax
import jax.numpy as jnp
from jax import lax
from jax.experimental import pallas as pl
from jax.experimental.pallas import tpu as pltpu
from jax.sharding import PartitionSpec as P

HEADS = 16
DK = 128
DV = 128
CHUNK = 128
LANES = 128
F32 = jnp.float32
BF16 = jnp.bfloat16


def halves(a):
    high = a.astype(BF16)
    return high, (a - high.astype(F32)).astype(BF16)


def contract(a, b, dims):
    return lax.dot_general(a, b, dims, preferred_element_type=F32)


def dot3(a, b, ca, cb, batch=0):
    ah, al = halves(a)
    bh, bl = halves(b)
    lead = tuple(range(batch))
    dims = (((ca,), (cb,)), (lead, lead))
    return contract(ah, bh, dims) + (contract(ah, bl, dims) + contract(al, bh, dims))


def block_kernel(
    heads, x_ref, w_ref, wg_ref, rate_ref, bias_ref, read_ref, query_ref, state_ref, cum, cum_row, beta
):
    head = pl.program_id(0)
    rows = x_ref.shape[0]
    chunks = rows // CHUNK
    row_at = lax.broadcasted_iota(jnp.int32, (CHUNK, CHUNK), 0)
    col_at = lax.broadcasted_iota(jnp.int32, (CHUNK, CHUNK), 1)

    @pl.when(head == 0)
    def _():
        logits = contract(x_ref[...], wg_ref[...], (((1,), (0,)), ((), ())))
        soft = jnp.maximum(logits, 0.0) + jnp.log1p(jnp.exp(-jnp.abs(logits)))
        decay = (-rate_ref[...] * soft).astype(BF16)
        beta[...] = (
            (1.0 / (1.0 + jnp.exp(-(logits + bias_ref[...])))).astype(BF16).astype(F32)
        ).reshape(chunks, CHUNK, LANES)
        lower_ones = jnp.where(row_at >= col_at, 1.0, 0.0).astype(BF16)
        for c in range(chunks):
            piece = decay[c * CHUNK : (c + 1) * CHUNK]
            sums = contract(lower_ones, piece, (((1,), (0,)), ((), ())))
            cum[c] = sums
            cum_row[c] = sums.T

    raw = contract(x_ref[...], w_ref[0], (((1,), (0,)), ((), ())))
    raw_q = raw[:, :DK]
    raw_k = raw[:, DK : 2 * DK]
    q = (
        raw_q * lax.rsqrt(jnp.sum(raw_q * raw_q, -1, keepdims=True) + 1e-06) * DK ** (-0.5)
    ).astype(BF16)
    k = (raw_k * lax.rsqrt(jnp.sum(raw_k * raw_k, -1, keepdims=True) + 1e-06)).astype(BF16)
    v = raw[:, 2 * DK :].astype(BF16)
    q = q.reshape(chunks, CHUNK, DK)
    k = k.reshape(chunks, CHUNK, DK)
    v = v.reshape(chunks, CHUNK, DV).astype(F32)

    lane = lax.broadcasted_iota(jnp.int32, (chunks, CHUNK, LANES), 2)
    g = jnp.sum(jnp.where(lane == head, cum[...], 0.0), -1, keepdims=True)
    b = jnp.sum(jnp.where(lane == head + heads, beta[...], 0.0), -1, keepdims=True)
    g_row = cum_row[:, pl.ds(head, 1), :]
    g_last = g[:, CHUNK - 1 :, :]
    growth = jnp.exp(g)
    tail = jnp.exp(g_last - g)
    whole = jnp.exp(g_last)

    batched = (((2,), (2,)), ((0,), (0,)))
    pair = contract(jnp.concatenate([k, q], 1), k, batched)
    low = row_at >= col_at
    spread = jnp.exp(jnp.where(low[None], g - g_row, 0.0))
    lmat = jnp.where((row_at > col_at)[None], b * spread * pair[:, :CHUNK], 0.0)
    mmat = jnp.where(low[None], spread * pair[:, CHUNK:], 0.0)

    eye = jnp.where(row_at == col_at, 1.0, 0.0)
    inverse = None
    size = 1
    while size < CHUNK:
        inside = (row_at // (2 * size) == col_at // (2 * size)) & (row_at // size != col_at // size)
        off = jnp.where(inside[None], lmat, 0.0)
        if inverse is None:
            inverse = eye[None] - off
        else:
            inverse = inverse - dot3(inverse, dot3(off, inverse, 2, 1, 1), 2, 1, 1)
        size *= 2

    kf = k.astype(F32)
    right = jnp.concatenate([(b * growth) * kf, b * v], 2)
    wu = dot3(inverse, right, 2, 1, 1)
    mwu = dot3(mmat, wu, 2, 1, 1)
    moved = growth * q.astype(F32) - mwu[:, :, :DK]
    key_tail = tail * kf
    jumps = dot3(jnp.swapaxes(wu, 1, 2), key_tail, 2, 1, 1)
    step_map = whole * eye[None] - jumps[:, :DK]

    carry = jnp.concatenate([step_map[0], jumps[0, DK:]], 0)
    query_ref[:CHUNK] = moved[0]
    read_ref[:CHUNK] = mwu[0, :, DK:]
    for c in range(1, chunks):
        both = dot3(moved[c], carry, 1, 1)
        at = slice(c * CHUNK, (c + 1) * CHUNK)
        query_ref[at] = both[:, :DK]
        read_ref[at] = mwu[c, :, DK:] + both[:, DK:]
        carry = dot3(carry, step_map[c], 1, 0)
        carry = jnp.concatenate([carry[:DK], carry[DK:] + jumps[c, DK:]], 0)
    state_ref[0] = carry


def tail_kernel(place_ref, read_ref, query_ref, maps_ref, gain_ref, out_ref):
    def step(lap, state):
        return dot3(state, maps_ref[lap, 0, :DK, :], 1, 0) + maps_ref[lap, 0, DK:, :]

    state = lax.fori_loop(0, place_ref[0], step, jnp.zeros((DV, DK), F32))
    read = read_ref[...] + dot3(query_ref[...], state, 1, 1)
    readout = read.astype(BF16).astype(F32)
    scale = lax.rsqrt(jnp.mean(readout * readout, -1, keepdims=True) + 1e-06)
    out_ref[...] = (readout * scale * gain_ref[...]).astype(BF16)


def shards(
    tokens, w_query, w_key, w_value, decay_proj, beta_proj, decay_rate, beta_bias, norm_gain
):
    streams = lax.axis_size("stream")
    places = lax.axis_size("tm")
    heads = HEADS // streams
    depth = w_query.shape[0]
    share = depth // places
    place = lax.axis_index("tm")
    stream = lax.axis_index("stream")

    def mine(w):
        return lax.dynamic_slice_in_dim(w, place * share, share, 0)

    pieces = jnp.stack(
        [mine(w).reshape(share, streams, heads, DK) for w in (w_query, w_key, w_value)], 3
    ).reshape(share, streams, heads * 3 * DK)
    gates = jnp.concatenate(
        [mine(w).reshape(share, streams, heads) for w in (decay_proj, beta_proj)], 2
    )
    gates = jnp.pad(gates, ((0, 0), (0, 0), (0, LANES - 2 * heads)))
    sent = jnp.concatenate([pieces, gates], 2).transpose(1, 0, 2)
    swapped = lax.all_to_all(sent, "stream", 0, 0, tiled=True)
    full = lax.all_gather(swapped, "tm", axis=0)
    full = full.transpose(1, 0, 2, 3).reshape(streams * depth, -1)
    w_heads = full[:, : heads * 3 * DK].reshape(streams * depth, heads, 3 * DK).transpose(1, 0, 2)
    w_gates = full[:, heads * 3 * DK :]
    x = lax.all_gather(tokens, "stream", axis=0, tiled=True)
    rows = x.shape[0]
    width = x.shape[1]

    rate = lax.dynamic_slice_in_dim(decay_rate, stream * heads, heads)
    bias = lax.dynamic_slice_in_dim(beta_bias, stream * heads, heads)
    rate = jnp.pad(rate, (0, LANES - heads))[None]
    bias = jnp.pad(bias, (heads, LANES - 2 * heads))[None]

    chunks = rows // CHUNK
    read, moved, maps = pl.pallas_call(
        functools.partial(block_kernel, heads),
        grid=(heads,),
        out_shape=(
            jax.ShapeDtypeStruct((rows, heads * DV), F32),
            jax.ShapeDtypeStruct((rows, heads * DK), F32),
            jax.ShapeDtypeStruct((heads, DK + DV, DK), F32),
        ),
        in_specs=[
            pl.BlockSpec((rows, width), lambda h: (0, 0)),
            pl.BlockSpec((1, width, 3 * DK), lambda h: (h, 0, 0)),
            pl.BlockSpec((width, LANES), lambda h: (0, 0)),
            pl.BlockSpec((1, LANES), lambda h: (0, 0)),
            pl.BlockSpec((1, LANES), lambda h: (0, 0)),
        ],
        out_specs=(
            pl.BlockSpec((rows, DV), lambda h: (0, h)),
            pl.BlockSpec((rows, DK), lambda h: (0, h)),
            pl.BlockSpec((1, DK + DV, DK), lambda h: (h, 0, 0)),
        ),
        scratch_shapes=[
            pltpu.VMEM((chunks, CHUNK, LANES), F32),
            pltpu.VMEM((chunks, LANES, CHUNK), F32),
            pltpu.VMEM((chunks, CHUNK, LANES), F32),
        ],
    )(x, w_heads, w_gates, rate, bias)

    gathered = lax.all_gather(maps, "tm", axis=0)
    mixed = pl.pallas_call(
        tail_kernel,
        grid=(heads,),
        out_shape=jax.ShapeDtypeStruct((rows, heads * DV), BF16),
        in_specs=[
            pl.BlockSpec(memory_space=pltpu.SMEM),
            pl.BlockSpec((rows, DV), lambda h: (0, h)),
            pl.BlockSpec((rows, DK), lambda h: (0, h)),
            pl.BlockSpec((places, 1, DK + DV, DK), lambda h: (0, h, 0, 0)),
            pl.BlockSpec((1, DV), lambda h: (0, 0)),
        ],
        out_specs=pl.BlockSpec((rows, DV), lambda h: (0, h)),
    )(place[None].astype(jnp.int32), read, moved, gathered, norm_gain[None])
    return lax.all_to_all(mixed, "stream", split_axis=0, concat_axis=1, tiled=True)


def solution(mesh):
    return jax.shard_map(
        shards,
        mesh=mesh,
        in_specs=(
            P(("tm", "stream"), None),
            P("stream", None),
            P("stream", None),
            P("stream", None),
            P("stream", None),
            P("stream", None),
            P(),
            P(),
            P(),
        ),
        out_specs=P(("tm", "stream"), None),
        check_vma=False,
    )
```

time: 682 us -> 233 us (0.34)
  waiting for transfers between devices: 355 us -> 120 us
  other arithmetic: 171 us -> 1.89 us
  matrix products: 50.9 us -> 0 us
  Pallas kernels: 0 us -> 35.6 us
  starting transfers between devices: 24 us -> 0.08 us
  local copies, waits for them, and re-layouts: 30.6 us -> 15.5 us
  blocking collectives: 33.7 us -> 46.5 us
    another operation x11 -> x1, other arithmetic: 163 us -> 0.66 us  [shards(): jnp.stack([mine(w).reshape(share, streams, heads, DK) for w in (w_query,...]
    all_gather x5 -> x3, waiting for transfers between devices: 267 us -> 119 us  [the longest x1 44.3 us: shards(): full = lax.all_gather(swapped, 'tm', axis=0)]
    all_to_all x6 -> x0, waiting for transfers between devices: 86.2 us -> none  [the longest x1 29.3 us: shards(): lax.all_to_all(values, 'stream', split_axis=1, concat_axis=0, tiled=True)]
    dot_general x23 -> x0, matrix products: 46.8 us -> none  [the longest x5 15.6 us: add_rows(): return jnp.dot(inputs, piece, preferred_element_type=jnp.float32)]
    all_to_all x0 -> x2, blocking collectives: none -> 46.5 us  [the longest x1 26.3 us: shards(): swapped = lax.all_to_all(sent, 'stream', 0, 0, tiled=True)]
    pallas_call x0 -> x2, Pallas kernels: none -> 35.6 us  [the longest x1 27.8 us: shards(): pl.pallas_call(functools.partial(block_kernel, heads), grid=(heads,), out...]
    all_gather x2 -> x0, blocking collectives: 33.7 us -> none  [the longest x1 20.2 us: shards(): lax.all_gather(beta_proj, 'stream', axis=0, tiled=True)]
    all_to_all x6 -> x0, starting transfers between devices: 23.6 us -> none  [the longest x1 4.64 us: shards(): lax.all_to_all(log_decay, 'stream', split_axis=1, concat_axis=0, tiled=True)]
  transfers between devices with their start and end apart: 11 -> 3, of which waited for: 7 -> 3; matrix products, arithmetic and copies ran while one was open for 33% -> 4% of each run, Pallas kernels for 0% -> 0%
where the time goes in v1:
time: 233 us; the launch traced here: 232 us
  waiting for transfers between devices  120 us (52%)
  blocking collectives  46.5 us (20%)
  Pallas kernels  35.6 us (15%)
  local copies, waits for them, and re-layouts  15.5 us (7%)
  between operations  13.2 us (6%)
    all_gather x1, waiting for transfers between devices, shards(): full = lax.all_gather(swapped, 'tm', axis=0)  44.3 us
    all_gather x1, waiting for transfers between devices, shards(): x = lax.all_gather(tokens, 'stream', axis=0, tiled=True)  40 us
    all_gather x1, waiting for transfers between devices, shards(): gathered = lax.all_gather(maps, 'tm', axis=0)  34.6 us
    pallas_call x1, Pallas kernels, shards(): pl.pallas_call(functools.partial(block_kernel, heads), grid=(heads,), out...  27.8 us
    all_to_all x1, blocking collectives, shards(): swapped = lax.all_to_all(sent, 'stream', 0, 0, tiled=True)  26.3 us
    all_to_all x1, blocking collectives, shards(): lax.all_to_all(mixed, 'stream', split_axis=0, concat_axis=1, tiled=True)  20.2 us
    pallas_call x1, Pallas kernels, shards(): pl.pallas_call(tail_kernel, grid=(heads,), out_shape=jax.ShapeDtypeStruct...  7.79 us
  transfers between devices with their start and end apart: 3, of which 3 were waited for; matrix products, arithmetic and copies ran while one was open for 4% of the time, Pallas kernels for 0%

profile of v1, /device:TPU:6, one launch (start us, length us, event | category | flops | bytes accessed | tf_op | source)
XLA Modules:
  0.0 232.4 jit_solution(15863303708298385563)
XLA Ops:
  6.5 0.0 copy-start
  6.5 0.0 all-gather.8.cloned.1.call-start
  6.5 0.9 constant_dynamic-slice_fusion
  7.5 0.1 copy.24
  7.6 0.6 copy-done
  8.2 0.2 stack_reshape.9
  8.4 1.1 constant_dynamic-slice_fusion.2
  9.4 0.2 stack_reshape.11
  9.6 0.2 stack_reshape.10
  9.8 0.7 pad_maximum_fusion
  10.4 1.1 copy.23
  11.5 1.5 reshape.18
  13.0 0.0 copy-start.1
  13.0 0.0 copy-start.2
  13.0 1.2 fusion.2
  14.2 26.3 %all_to_all.24 = bf16[4,64,1664]{2,1,0:T(8,128)(2,1)} all-to-all(bf16[4,64,1664]{2,1,0:T(8,128)(2,1)S(1)} %fusion.2), channel_id=1, replica_groups=mesh['tm'=8,'stream'=4] {'stream'}, dimensions={0} | all-to-all | bytes 1703936 | tf_op jit(solution)/shard_map/all_to_all | solution.py:155
  40.5 0.0 all-gather.8.cloned.1.call-update
  40.5 0.0 all-gather.6.cloned.1.call-start
  40.6 0.7 all-gather.6.cloned.1.call-update
  41.3 0.0 all-gather.10.cloned.1.call-start
  41.3 0.0 copy-done.1
  41.3 0.1 dynamic_slice.26
  41.4 0.0 copy-done.2
  41.4 0.1 dynamic_slice.27
  41.5 0.7 pad_bitcast_fusion
  42.2 44.3 %all-gather.8.cloned.1.call-done = bf16[32,64,1664]{2,1,0:T(8,128)(2,1)} async-done(((bf16[4,64,1664]{2,1,0:T(8,128)(2,1)}), bf16[32,64,1664]{2,1,0:T(8,128)(2,1)}) %all-gather.8.cloned.1.call-update) | async-done | bytes 6815760 | tf_op jit(solution)/shard_map/all_gather | solution.py:156
  86.4 3.5 %copy.25 = bf16[4,8,64,1664]{3,2,1,0:T(8,128)(2,1)S(1)} copy(bf16[4,8,64,1664]{3,2,0,1:T(8,128)(2,1)} %bitcast.32) | data formatting | bytes 13631488 | tf_op jit(solution)/shard_map/transpose | solution.py:157
  89.9 0.8 slice.9.wg_ref
  90.8 0.5 slice.8
  91.3 3.3 %copy.31 = bf16[256,4,8,384]{3,2,0,1:T(8,128)(2,1)} copy(bf16[256,4,8,384]{3,2,1,0:T(8,128)(2,1)S(1)} %bitcast.31) | data formatting | bytes 12582912 | tf_op jit(solution)/shard_map/reshape | solution.py:158
  94.5 40.0 %all-gather.6.cloned.1.call-done.x_ref = bf16[512,2048]{1,0:T(8,128)(2,1)} async-done(((bf16[128,2048]{1,0:T(8,128)(2,1)}), bf16[512,2048]{1,0:T(8,128)(2,1)}) %all-gather.6.cloned.1.call-update) | async-done | bytes 2097168 | tf_op jit(solution)/shard_map/all_gather | solution.py:160
  134.6 27.8 %shard_map.91 = (f32[512,512]{1,0:T(8,128)}, f32[512,512]{1,0:T(8,128)}, f32[4,256,128]{2,1,0:T(8,128)}) custom-call(bf16[512,2048]{1,0:T(8,128)(2,1)} %all-gather.6.cloned.1.call-done.x_ref, bf16[4,2048,384]{2,1,0:T(8,128)(2,1)} %bitcast.30, bf16[2048,128]{1,0:T(8,128)(2,1)} %slice.9.wg_ref, f32[1,128]{1,0:T(1,128)} %get-tuple-element.16.rate_ref, ...), custom_call_target="tpu_custom_call" | custom-call | tf_op jit(solution)/shard_map/pallas_call | solution.py:170
  162.4 0.0 all-gather.10.cloned.1.call-update
  162.4 34.6 %all-gather.10.cloned.1.call-done = f32[32,256,128]{2,1,0:T(8,128)} async-done(((f32[4,256,128]{2,1,0:T(8,128)}), f32[32,256,128]{2,1,0:T(8,128)}) %all-gather.10.cloned.1.call-update) | async-done | bytes 4194320 | tf_op jit(solution)/shard_map/all_gather | solution.py:197
  197.0 7.8 %shard_map.92 = bf16[512,512]{1,0:T(8,128)(2,1)} custom-call(s32[1]{0:T(128)} %bitcast.place_ref, f32[512,512]{1,0:T(8,128)} %get-tuple-element.8.read_ref, f32[512,512]{1,0:T(8,128)} %get-tuple-element.9.query_ref, f32[8,4,256,128]{3,2,1,0:T(8,128)} %bitcast.33, f32[1,128]{1,0:T(1,128)} %bitcast.38), custom_call_target="tpu_custom_call" | custom-call | tf_op jit(solution)/shard_map/pallas_call | solution.py:198
  204.8 20.2 %all_to_all.25 = bf16[4,128,512]{2,1,0:T(8,128)(2,1)S(1)} all-to-all(bf16[4,128,512]{2,1,0:T(8,128)(2,1)} %bitcast.34), channel_id=1, replica_groups=mesh['tm'=8,'stream'=4] {'stream'}, dimensions={0} | all-to-all | bytes 1048576 | tf_op jit(solution)/shard_map/all_to_all | solution.py:211
  225.0 0.8 copy.29
  (2 shorter events, 0.0 us)
Async XLA Ops:
  6.5 1.6 copy-start
  6.5 79.9 %all-gather.8.cloned.1.call-start = ((), (), s32[]{:S(2)}) async-start(), calls=%async_computation.3 | async-start | bytes 7667712 | tf_op jit(solution)/shard_map/all_gather | solution.py:156
  13.0 28.4 %copy-start.1 = (f32[16]{0:T(128)S(1)}, f32[16]{0:T(128)}, u32[]{:S(2)}) copy-start(f32[16]{0:T(128)} %param.15) | copy-start | bytes 196
  13.0 28.4 %copy-start.2 = (f32[16]{0:T(128)S(1)}, f32[16]{0:T(128)}, u32[]{:S(2)}) copy-start(f32[16]{0:T(128)} %param.16) | copy-start | bytes 196
  40.5 94.1 %all-gather.6.cloned.1.call-start = ((), (), s32[]{:S(2)}) async-start(), calls=%async_computation.2 | async-start | bytes 2621440 | tf_op jit(solution)/shard_map/all_gather | solution.py:160
  41.3 155.8 %all-gather.10.cloned.1.call-start = ((), (), s32[]{:S(2)}) async-start(), calls=%async_computation.4 | async-start | bytes 4718592 | tf_op jit(solution)/shard_map/all_gather | solution.py:197
Sparse Core Ops, SparseCore 0:
  40.7 45.7 all-gather.7
  88.0 46.5 all-gather.5
  162.5 34.4 all-gather.9

commit v2 on v1

--- a/solution.py
+++ b/solution.py
@@ -33,18 +33,240 @@
     return contract(ah, bh, dims) + (contract(ah, bl, dims) + contract(al, bh, dims))
 
 
+def around(count):
+    return sorted(range(1, count), key=lambda i: min(i, count - i))
+
+
+def gather_kernel(
+    streams,
+    places,
+    heads,
+    tok_ref,
+    wq_ref,
+    wk_ref,
+    wv_ref,
+    wg_ref,
+    x_ref,
+    full_ref,
+    stage,
+    load_sem,
+    own_sem,
+    tok_recv,
+    right_sem,
+    left_sem,
+    cross_send,
+    cross_recv,
+    plane_send,
+    pass_send,
+    plane_recv,
+):
+    t = lax.axis_index("tm")
+    z = lax.axis_index("stream")
+    chips = places // 2
+    chip = t // 2
+    core = t % 2
+    group = heads * DK
+
+    loads = []
+    for dest in range(streams):
+        for j, ref in enumerate((wq_ref, wk_ref, wv_ref)):
+            loads.append(
+                pltpu.make_async_copy(
+                    ref.at[t, :, pl.ds(dest * group, group)],
+                    stage.at[dest, :, pl.ds(j * group, group)],
+                    load_sem.at[dest, j],
+                )
+            )
+        loads.append(
+            pltpu.make_async_copy(
+                wg_ref.at[t], stage.at[dest, :, pl.ds(3 * group, LANES)], load_sem.at[dest, 3]
+            )
+        )
+    for copy in loads:
+        copy.start()
+
+    others = [(lax.rem(chip + i, chips) * 2 + core) for i in range(1, chips)]
+    sibling = chip * 2 + 1 - core
+    peers = [(t, lax.rem(z + i, streams)) for i in around(streams)]
+    peers += [(sibling, z)] + [(o, z) for o in others]
+    barrier = pltpu.get_barrier_semaphore()
+    for peer in peers:
+        pl.semaphore_signal(
+            barrier, inc=1, device_id=peer, device_id_type=pl.DeviceIdType.MESH
+        )
+    pl.semaphore_wait(barrier, len(peers))
+    for copy in loads:
+        copy.wait()
+
+    def remote(src, dst, send, recv, device):
+        return pltpu.make_async_remote_copy(
+            src_ref=src,
+            dst_ref=dst,
+            send_sem=send,
+            recv_sem=recv,
+            device_id=device,
+            device_id_type=pl.DeviceIdType.MESH,
+        )
+
+    def cross(i):
+        dest = lax.rem(z + i, streams)
+        return remote(
+            stage.at[dest], full_ref.at[t, z], cross_send.at[dest], cross_recv.at[z], (t, dest)
+        )
+
+    def crossed(i):
+        s = lax.rem(z + i, streams)
+        return remote(
+            stage.at[s], full_ref.at[t, s], cross_send.at[s], cross_recv.at[s], (t, s)
+        )
+
+    def line(chunk, right, first):
+        src = tok_ref if first else x_ref.at[chunk]
+        send = (right_sem if right else left_sem).at[chunk]
+        return remote(
+            src, x_ref.at[chunk], send, tok_recv.at[chunk], (t, z + 1 if right else z - 1)
+        )
+
+    def plane(i, s, first):
+        to = sibling if i == 0 else others[i - 1]
+        src = stage.at[z] if first else full_ref.at[t, s]
+        return remote(
+            src, full_ref.at[t, s], plane_send.at[i, s], plane_recv.at[t, s], (to, z)
+        )
+
+    def relay(i, s):
+        at = others[i - 1]
+        here = full_ref.at[at, s]
+        return remote(here, here, pass_send.at[i, s], plane_recv.at[at, s], (sibling, z))
+
+    def landed(at, s):
+        here = full_ref.at[at, s]
+        return remote(here, here, plane_send.at[0, s], plane_recv.at[at, s], (sibling, z))
+
+    for i in around(streams):
+        cross(i).start()
+
+    @pl.when(z < streams - 1)
+    def _():
+        line(z, True, True).start()
+
+    @pl.when(z > 0)
+    def _():
+        line(z, False, True).start()
+
+    for i in range(1, chips):
+        plane(i, z, True).start()
+    plane(0, z, True).start()
+    own = [
+        pltpu.make_async_copy(stage.at[z], full_ref.at[t, z], own_sem.at[0]),
+        pltpu.make_async_copy(tok_ref, x_ref.at[z], own_sem.at[1]),
+    ]
+    for copy in own:
+        copy.start()
+
+    for i in around(streams):
+        s = lax.rem(z + i, streams)
+        crossed(i).wait_recv()
+        for j in range(1, chips):
+            plane(j, s, False).start()
+        plane(0, s, False).start()
+
+    def step(k):
+        @pl.when(z >= k)
+        def _():
+            line(z - k, True, False).wait_recv()
+
+            @pl.when(z < streams - 1)
+            def _():
+                line(z - k, True, False).start()
+
+        @pl.when(z + k < streams)
+        def _():
+            line(z + k, False, False).wait_recv()
+
+            @pl.when(z > 0)
+            def _():
+                line(z + k, False, False).start()
+
+    orders = [z] + [lax.rem(z + i, streams) for i in around(streams)]
+    passed = 0
+    for k in range(1, streams):
+        step(k)
+        upto = len(orders) if k == streams - 2 else passed + 1
+        while passed < min(upto, len(orders)):
+            s = orders[passed]
+            for i in range(1, chips):
+                landed(others[i - 1], s).wait_recv()
+                relay(i, s).start()
+            passed += 1
+    while passed < len(orders):
+        s = orders[passed]
+        for i in range(1, chips):
+            landed(others[i - 1], s).wait_recv()
+            relay(i, s).start()
+        passed += 1
+
+    for copy in own:
+        copy.wait()
+    for s in orders:
+        landed(sibling, s).wait_recv()
+        for i in range(1, chips):
+            landed(lax.rem(chip + i, chips) * 2 + 1 - core, s).wait_recv()
+    for i in around(streams):
+        cross(i).wait_send()
+    for n, s in enumerate(orders):
+        for i in range(chips):
+            plane(i, s, n == 0).wait_send()
+        for i in range(1, chips):
+            relay(i, s).wait_send()
+    for k in range(streams):
+
+        @pl.when((z >= k) & (z < streams - 1))
+        def _():
+            line(z - k, True, k == 0).wait_send()
+
+        @pl.when((z + k < streams) & (z > 0))
+        def _():
+            line(z + k, False, k == 0).wait_send()
+
+
 def block_kernel(
-    heads, x_ref, w_ref, wg_ref, rate_ref, bias_ref, read_ref, query_ref, state_ref, cum, cum_row, beta
+    heads,
+    x_ref,
+    wq_ref,
+    wk_ref,
+    wv_ref,
+    wg_ref,
+    rate_ref,
+    bias_ref,
+    read_ref,
+    query_ref,
+    state_ref,
+    cum,
+    cum_row,
+    beta,
 ):
-    head = pl.program_id(0)
+    first_head = lax.axis_index("stream") * heads
+    head = pl.program_id(0) + first_head
     rows = x_ref.shape[0]
+    places, streams, share, _ = wq_ref.shape
+    depth = places * share
+
+    def project(refs):
+        total = None
+        for s in range(streams):
+            w = jnp.concatenate([ref[:, s].reshape(depth, LANES) for ref in refs], 1)
+            term = contract(x_ref[:, s * depth : (s + 1) * depth], w, (((1,), (0,)), ((), ())))
+            total = term if total is None else total + term
+        return total
+
     chunks = rows // CHUNK
     row_at = lax.broadcasted_iota(jnp.int32, (CHUNK, CHUNK), 0)
     col_at = lax.broadcasted_iota(jnp.int32, (CHUNK, CHUNK), 1)
 
-    @pl.when(head == 0)
+    @pl.when(pl.program_id(0) == 0)
     def _():
-        logits = contract(x_ref[...], wg_ref[...], (((1,), (0,)), ((), ())))
+        logits = project((wg_ref,))
         soft = jnp.maximum(logits, 0.0) + jnp.log1p(jnp.exp(-jnp.abs(logits)))
         decay = (-rate_ref[...] * soft).astype(BF16)
         beta[...] = (
@@ -57,7 +279,7 @@
             cum[c] = sums
             cum_row[c] = sums.T
 
-    raw = contract(x_ref[...], w_ref[0], (((1,), (0,)), ((), ())))
+    raw = project((wq_ref, wk_ref, wv_ref))
     raw_q = raw[:, :DK]
     raw_k = raw[:, DK : 2 * DK]
     q = (
@@ -71,7 +293,7 @@
 
     lane = lax.broadcasted_iota(jnp.int32, (chunks, CHUNK, LANES), 2)
     g = jnp.sum(jnp.where(lane == head, cum[...], 0.0), -1, keepdims=True)
-    b = jnp.sum(jnp.where(lane == head + heads, beta[...], 0.0), -1, keepdims=True)
+    b = jnp.sum(jnp.where(lane == head + HEADS, beta[...], 0.0), -1, keepdims=True)
     g_row = cum_row[:, pl.ds(head, 1), :]
     g_last = g[:, CHUNK - 1 :, :]
     growth = jnp.exp(g)
@@ -139,32 +361,45 @@
     depth = w_query.shape[0]
     share = depth // places
     place = lax.axis_index("tm")
-    stream = lax.axis_index("stream")
-
-    def mine(w):
-        return lax.dynamic_slice_in_dim(w, place * share, share, 0)
-
-    pieces = jnp.stack(
-        [mine(w).reshape(share, streams, heads, DK) for w in (w_query, w_key, w_value)], 3
-    ).reshape(share, streams, heads * 3 * DK)
-    gates = jnp.concatenate(
-        [mine(w).reshape(share, streams, heads) for w in (decay_proj, beta_proj)], 2
+    width = 3 * heads * DK + LANES
+    gates = jnp.pad(
+        jnp.concatenate([decay_proj, beta_proj], 1), ((0, 0), (0, LANES - 2 * HEADS))
     )
-    gates = jnp.pad(gates, ((0, 0), (0, 0), (0, LANES - 2 * heads)))
-    sent = jnp.concatenate([pieces, gates], 2).transpose(1, 0, 2)
-    swapped = lax.all_to_all(sent, "stream", 0, 0, tiled=True)
-    full = lax.all_gather(swapped, "tm", axis=0)
-    full = full.transpose(1, 0, 2, 3).reshape(streams * depth, -1)
-    w_heads = full[:, : heads * 3 * DK].reshape(streams * depth, heads, 3 * DK).transpose(1, 0, 2)
-    w_gates = full[:, heads * 3 * DK :]
-    x = lax.all_gather(tokens, "stream", axis=0, tiled=True)
+    shares = [w.reshape(places, share, -1) for w in (w_query, w_key, w_value, gates)]
+    local, features = tokens.shape
+    any_space = pl.BlockSpec(memory_space=pl.ANY)
+    dma = pltpu.SemaphoreType.DMA
+    chips = places // 2
+    x, full = pl.pallas_call(
+        functools.partial(gather_kernel, streams, places, heads),
+        out_shape=(
+            jax.ShapeDtypeStruct((streams, local, features), BF16),
+            jax.ShapeDtypeStruct((places, streams, share, width), BF16),
+        ),
+        in_specs=[pl.BlockSpec(memory_space=pltpu.VMEM)] + [any_space] * 4,
+        out_specs=(any_space, any_space),
+        scratch_shapes=[
+            pltpu.VMEM((streams, share, width), BF16),
+            dma((streams, 4)),
+            dma((2,)),
+            dma((streams,)),
+            dma((streams,)),
+            dma((streams,)),
+            dma((streams,)),
+            dma((streams,)),
+            dma((chips, streams)),
+            dma((chips, streams)),
+            dma((places, streams)),
+        ],
+        compiler_params=pltpu.CompilerParams(collective_id=0, has_side_effects=True),
+    )(tokens, *shares)
+    x = x.reshape(streams * local, features)
     rows = x.shape[0]
-    width = x.shape[1]
-
-    rate = lax.dynamic_slice_in_dim(decay_rate, stream * heads, heads)
-    bias = lax.dynamic_slice_in_dim(beta_bias, stream * heads, heads)
-    rate = jnp.pad(rate, (0, LANES - heads))[None]
-    bias = jnp.pad(bias, (heads, LANES - 2 * heads))[None]
+    if share % 16:
+        full = full.transpose(1, 0, 2, 3).reshape(1, streams, places * share, width)
+
+    rate = jnp.pad(decay_rate, (0, LANES - HEADS))[None]
+    bias = jnp.pad(beta_bias, (HEADS, LANES - 2 * HEADS))[None]
 
     chunks = rows // CHUNK
     read, moved, maps = pl.pallas_call(
@@ -176,9 +411,11 @@
             jax.ShapeDtypeStruct((heads, DK + DV, DK), F32),
         ),
         in_specs=[
-            pl.BlockSpec((rows, width), lambda h: (0, 0)),
-            pl.BlockSpec((1, width, 3 * DK), lambda h: (h, 0, 0)),
-            pl.BlockSpec((width, LANES), lambda h: (0, 0)),
+            pl.BlockSpec((rows, features), lambda h: (0, 0)),
+            pl.BlockSpec(full.shape[:3] + (DK,), lambda h: (0, 0, 0, h)),
+            pl.BlockSpec(full.shape[:3] + (DK,), lambda h: (0, 0, 0, heads + h)),
+            pl.BlockSpec(full.shape[:3] + (DV,), lambda h: (0, 0, 0, 2 * heads + h)),
+            pl.BlockSpec(full.shape[:3] + (LANES,), lambda h: (0, 0, 0, 3 * heads)),
             pl.BlockSpec((1, LANES), lambda h: (0, 0)),
             pl.BlockSpec((1, LANES), lambda h: (0, 0)),
         ],
@@ -192,7 +429,7 @@
             pltpu.VMEM((chunks, LANES, CHUNK), F32),
             pltpu.VMEM((chunks, CHUNK, LANES), F32),
         ],
-    )(x, w_heads, w_gates, rate, bias)
+    )(x, full, full, full, full, rate, bias)
 
     gathered = lax.all_gather(maps, "tm", axis=0)
     mixed = pl.pallas_call(

time: 233 us -> 169 us (0.73)
  waiting for transfers between devices: 120 us -> 35.6 us
  Pallas kernels: 35.6 us -> 95.6 us
  blocking collectives: 46.5 us -> 20.2 us
  local copies, waits for them, and re-layouts: 15.5 us -> 2.92 us
    all_gather x2 -> x0, waiting for transfers between devices: 84.3 us -> none  [the longest x1 44.3 us: shards(): full = lax.all_gather(swapped, 'tm', axis=0)]
    pallas_call x0 -> x1, Pallas kernels: none -> 59.6 us  [shards(): pl.pallas_call(functools.partial(gather_kernel, streams, places, heads),...]
    all_to_all x1 -> x0, blocking collectives: 26.3 us -> none  [shards(): swapped = lax.all_to_all(sent, 'stream', 0, 0, tiled=True)]
    reshape x2 -> x0, local copies, waits for them, and re-layouts: 4.74 us -> none  [the longest x1 3.28 us: shards(): full[:, :heads * 3 * DK].reshape(streams * depth, heads, 3 * DK)]
    transpose x1 -> x0, local copies, waits for them, and re-layouts: 3.52 us -> none  [shards(): full = full.transpose(1, 0, 2, 3).reshape(streams * depth, -1)]
  transfers between devices with their start and end apart: 3 -> 1, of which waited for: 3 -> 1; matrix products, arithmetic and copies ran while one was open for 4% -> 0% of each run, Pallas kernels for 0% -> 0%
where the time goes in v2:
time: 169 us; the launch traced here: 168 us
  Pallas kernels  95.6 us (57%)
  waiting for transfers between devices  35.6 us (21%)
  blocking collectives  20.2 us (12%)
  between operations  13.4 us (8%)
  local copies, waits for them, and re-layouts  2.92 us (2%)
    pallas_call x1, Pallas kernels, shards(): pl.pallas_call(functools.partial(gather_kernel, streams, places, heads),...  59.6 us
    all_gather x1, waiting for transfers between devices, shards(): gathered = lax.all_gather(maps, 'tm', axis=0)  35.6 us
    pallas_call x1, Pallas kernels, shards(): pl.pallas_call(functools.partial(block_kernel, heads), grid=(heads,), out...  28.1 us
    all_to_all x1, blocking collectives, shards(): lax.all_to_all(mixed, 'stream', split_axis=0, concat_axis=1, tiled=True)  20.2 us
    pallas_call x1, Pallas kernels, shards(): pl.pallas_call(tail_kernel, grid=(heads,), out_shape=jax.ShapeDtypeStruct...  7.79 us
  transfers between devices with their start and end apart: 1, of which 1 were waited for; matrix products, arithmetic and copies ran while one was open for 0% of the time, Pallas kernels for 0%

profile of v2, /device:TPU:6, one launch (start us, length us, event | category | flops | bytes accessed | tf_op | source)
XLA Modules:
  0.0 168.4 jit_solution(15841435087540427403)
XLA Ops:
  6.5 0.0 all-gather.3.cloned.1.call-start
  6.5 0.7 pad_maximum_fusion
  7.3 0.1 copy.14
  7.4 0.7 pad.12.clone
  8.1 1.3 pad_bitcast_fusion
  9.4 59.6 %shard_map.91 = (bf16[4,128,2048]{2,1,0:T(8,128)(2,1)}, bf16[8,4,64,1664]{3,2,1,0:T(8,128)(2,1)}) custom-call(bf16[128,2048]{1,0:T(8,128)(2,1)} %tok_ref.1, bf16[8,64,2048]{2,1,0:T(8,128)(2,1)} %bitcast.19, bf16[8,64,2048]{2,1,0:T(8,128)(2,1)} %bitcast.20, bf16[8,64,2048]{2,1,0:T(8,128)(2,1)} %bitcast.21, bf16[8,64,128]{2,1,0:T(8,128)(2,1)} %bitcast.23), custom_call_target="tpu_custom_call" | custom-call | tf_op jit(solution)/shard_map/pallas_call | solution.py:373
  69.0 28.1 %shard_map.92 = (f32[512,512]{1,0:T(8,128)}, f32[512,512]{1,0:T(8,128)}, f32[4,256,128]{2,1,0:T(8,128)}) custom-call(bf16[512,2048]{1,0:T(8,128)(2,1)} %bitcast.17, bf16[8,4,64,1664]{3,2,1,0:T(8,128)(2,1)} %get-tuple-element.11.wq_ref.wk_ref.wv_ref.wg_ref, bf16[8,4,64,1664]{3,2,1,0:T(8,128)(2,1)} %get-tuple-element.11.wq_ref.wk_ref.wv_ref.wg_ref, ...), custom_call_target="tpu_custom_call" | custom-call | tf_op jit(solution)/shard_map/pallas_call | solution.py:405
  97.1 0.0 all-gather.3.cloned.1.call-update
  97.2 35.6 %all-gather.3.cloned.1.call-done = f32[32,256,128]{2,1,0:T(8,128)} async-done(((f32[4,256,128]{2,1,0:T(8,128)}), f32[32,256,128]{2,1,0:T(8,128)}) %all-gather.3.cloned.1.call-update) | async-done | bytes 4194320 | tf_op jit(solution)/shard_map/all_gather | solution.py:434
  132.7 7.8 %shard_map.93 = bf16[512,512]{1,0:T(8,128)(2,1)} custom-call(s32[1]{0:T(128)} %bitcast.place_ref, f32[512,512]{1,0:T(8,128)} %get-tuple-element.12.read_ref, f32[512,512]{1,0:T(8,128)} %get-tuple-element.13.query_ref, f32[8,4,256,128]{3,2,1,0:T(8,128)} %bitcast.16, f32[1,128]{1,0:T(1,128)} %bitcast.24), custom_call_target="tpu_custom_call" | custom-call | tf_op jit(solution)/shard_map/pallas_call | solution.py:435
  140.5 20.2 %all_to_all.19 = bf16[4,128,512]{2,1,0:T(8,128)(2,1)S(1)} all-to-all(bf16[4,128,512]{2,1,0:T(8,128)(2,1)} %bitcast.18), channel_id=1, replica_groups=mesh['tm'=8,'stream'=4] {'stream'}, dimensions={0} | all-to-all | bytes 1048576 | tf_op jit(solution)/shard_map/all_to_all | solution.py:448
  160.7 0.8 copy.15
Async XLA Ops:
  6.5 126.2 %all-gather.3.cloned.1.call-start = ((), (), s32[]{:S(2)}) async-start(), calls=%async_computation.1 | async-start | bytes 4718592 | tf_op jit(solution)/shard_map/all_gather | solution.py:434
Sparse Core Ops, SparseCore 0:
  97.3 35.4 all-gather.2

commit v3 on v2

--- a/solution.py
+++ b/solution.py
@@ -341,15 +341,169 @@
     state_ref[0] = carry
 
 
-def tail_kernel(place_ref, read_ref, query_ref, maps_ref, gain_ref, out_ref):
-    def step(lap, state):
-        return dot3(state, maps_ref[lap, 0, :DK, :], 1, 0) + maps_ref[lap, 0, DK:, :]
-
-    state = lax.fori_loop(0, place_ref[0], step, jnp.zeros((DV, DK), F32))
-    read = read_ref[...] + dot3(query_ref[...], state, 1, 1)
-    readout = read.astype(BF16).astype(F32)
-    scale = lax.rsqrt(jnp.mean(readout * readout, -1, keepdims=True) + 1e-06)
-    out_ref[...] = (readout * scale * gain_ref[...]).astype(BF16)
+def return_kernel(
+    streams,
+    places,
+    heads,
+    read_ref,
+    query_ref,
+    maps_ref,
+    gain_ref,
+    out_ref,
+    pair,
+    total,
+    got,
+    carried,
+    state,
+    mixed,
+    pair_sem,
+    state_sem,
+    chip_send,
+    chip_recv,
+    out_send,
+    out_recv,
+    own_sem,
+):
+    t = lax.axis_index("tm")
+    z = lax.axis_index("stream")
+    chips = places // 2
+    chip = t // 2
+    core = t % 2
+    sibling = chip * 2 + 1 - core
+    group = heads * DV
+    local = out_ref.shape[0]
+
+    peers = [(t, lax.rem(z + i, streams)) for i in around(streams)]
+    peers += [(sibling, z)]
+    peers += [(lax.rem(chip + i, chips) * 2 + core, z) for i in range(1, chips)]
+    barrier = pltpu.get_barrier_semaphore()
+    for peer in peers:
+        pl.semaphore_signal(
+            barrier, inc=1, device_id=peer, device_id_type=pl.DeviceIdType.MESH
+        )
+    pl.semaphore_wait(barrier, len(peers))
+
+    def remote(src, dst, send, recv, device):
+        return pltpu.make_async_remote_copy(
+            src_ref=src,
+            dst_ref=dst,
+            send_sem=send,
+            recv_sem=recv,
+            device_id=device,
+            device_id_type=pl.DeviceIdType.MESH,
+        )
+
+    def hand_over():
+        return remote(maps_ref, pair, pair_sem.at[0], pair_sem.at[1], (sibling, z))
+
+    def hand_back():
+        return remote(carried, carried, state_sem.at[0], state_sem.at[1], (sibling, z))
+
+    def to_chip(source, dest):
+        src, dst = total, got.at[source]
+        if source == 0:
+            src, dst = total.at[:, pl.ds(DK, DV)], got.at[0, :, pl.ds(DK, DV)]
+        return remote(src, dst, chip_send.at[dest], chip_recv.at[source], (dest * 2 + 1, z))
+
+    @pl.when(core == 0)
+    def _():
+        hand_over().start()
+        hand_over().wait_send()
+
+    @pl.when(core == 1)
+    def _():
+        hand_over().wait_recv()
+
+        @pl.when(chip < chips - 1)
+        def _():
+            for h in range(heads):
+                both = dot3(pair[h], maps_ref[h, :DK], 1, 0)
+                total[h, :DK] = both[:DK]
+                total[h, DK:] = both[DK:] + maps_ref[h, DK:]
+
+        for source in range(chips - 1):
+
+            @pl.when(chip == source)
+            def _():
+                for dest in range(chips - 1, source, -1):
+                    to_chip(source, dest).start()
+
+        for source in range(chips - 1):
+
+            @pl.when(chip > source)
+            def _():
+                to_chip(source, chip).wait_recv()
+                for h in range(heads):
+                    if source == 0:
+                        carried[h] = got[0, h, DK:]
+                    else:
+                        carried[h] = dot3(carried[h], got[source, h, :DK], 1, 0) + got[source, h, DK:]
+
+        @pl.when(chip > 0)
+        def _():
+            hand_back().start()
+            for h in range(heads):
+                state[h] = dot3(carried[h], pair[h, :DK], 1, 0) + pair[h, DK:]
+
+        @pl.when(chip == 0)
+        def _():
+            for h in range(heads):
+                state[h] = pair[h, DK:]
+
+    @pl.when((core == 0) & (chip > 0))
+    def _():
+        hand_back().wait_recv()
+        for h in range(heads):
+            state[h] = carried[h]
+
+    @pl.when((core == 0) & (chip == 0))
+    def _():
+        state[...] = jnp.zeros_like(state)
+
+    def outgoing(i):
+        dest = lax.rem(z + i, streams)
+        dst = out_ref.at[:, pl.ds(pl.multiple_of(z * group, group), group)]
+        return remote(mixed.at[dest], dst, out_send.at[dest], out_recv.at[z], (t, dest))
+
+    def incoming(i):
+        source = lax.rem(z + i, streams)
+        dst = out_ref.at[:, pl.ds(pl.multiple_of(source * group, group), group)]
+        return remote(mixed.at[source], dst, out_send.at[source], out_recv.at[source], (t, source))
+
+    own = pltpu.make_async_copy(
+        mixed.at[z], out_ref.at[:, pl.ds(pl.multiple_of(z * group, group), group)], own_sem.at[0]
+    )
+    order = list(reversed(around(streams)))
+    for i in order + [0]:
+        dest = lax.rem(z + i, streams)
+        at = pl.ds(pl.multiple_of(dest * local, local), local)
+        for h in range(heads):
+            lanes = slice(h * DV, (h + 1) * DV)
+            read = read_ref[at, lanes] + dot3(query_ref[at, lanes], state[h], 1, 1)
+            readout = read.astype(BF16).astype(F32)
+            scale = lax.rsqrt(jnp.mean(readout * readout, -1, keepdims=True) + 1e-06)
+            mixed[dest, :, lanes] = (readout * scale * gain_ref[...]).astype(BF16)
+        if i == 0:
+            own.start()
+        else:
+            outgoing(i).start()
+
+    own.wait()
+    for i in order:
+        incoming(i).wait_recv()
+    for i in order:
+        outgoing(i).wait_send()
+
+    @pl.when((core == 1) & (chip > 0))
+    def _():
+        hand_back().wait_send()
+
+    for source in range(chips - 1):
+
+        @pl.when((core == 1) & (chip == source))
+        def _():
+            for dest in range(chips - 1, source, -1):
+                to_chip(source, dest).wait_send()
 
 
 def shards(
@@ -360,7 +514,6 @@
     heads = HEADS // streams
     depth = w_query.shape[0]
     share = depth // places
-    place = lax.axis_index("tm")
     width = 3 * heads * DK + LANES
     gates = jnp.pad(
         jnp.concatenate([decay_proj, beta_proj], 1), ((0, 0), (0, LANES - 2 * HEADS))
@@ -431,21 +584,29 @@
         ],
     )(x, full, full, full, full, rate, bias)
 
-    gathered = lax.all_gather(maps, "tm", axis=0)
-    mixed = pl.pallas_call(
-        tail_kernel,
-        grid=(heads,),
-        out_shape=jax.ShapeDtypeStruct((rows, heads * DV), BF16),
-        in_specs=[
-            pl.BlockSpec(memory_space=pltpu.SMEM),
-            pl.BlockSpec((rows, DV), lambda h: (0, h)),
-            pl.BlockSpec((rows, DK), lambda h: (0, h)),
-            pl.BlockSpec((places, 1, DK + DV, DK), lambda h: (0, h, 0, 0)),
-            pl.BlockSpec((1, DV), lambda h: (0, 0)),
+    vmem = pl.BlockSpec(memory_space=pltpu.VMEM)
+    return pl.pallas_call(
+        functools.partial(return_kernel, streams, places, heads),
+        out_shape=jax.ShapeDtypeStruct((local, HEADS * DV), BF16),
+        in_specs=[vmem] * 4,
+        out_specs=any_space,
+        scratch_shapes=[
+            pltpu.VMEM((heads, DK + DV, DK), F32),
+            pltpu.VMEM((heads, DK + DV, DK), F32),
+            pltpu.VMEM((chips, heads, DK + DV, DK), F32),
+            pltpu.VMEM((heads, DV, DK), F32),
+            pltpu.VMEM((heads, DV, DK), F32),
+            pltpu.VMEM((streams, local, heads * DV), BF16),
+            dma((2,)),
+            dma((2,)),
+            dma((chips,)),
+            dma((chips,)),
+            dma((streams,)),
+            dma((streams,)),
+            dma((1,)),
         ],
-        out_specs=pl.BlockSpec((rows, DV), lambda h: (0, h)),
-    )(place[None].astype(jnp.int32), read, moved, gathered, norm_gain[None])
-    return lax.all_to_all(mixed, "stream", split_axis=0, concat_axis=1, tiled=True)
+        compiler_params=pltpu.CompilerParams(collective_id=1, has_side_effects=True),
+    )(read, moved, maps, norm_gain[None])
 
 
 def solution(mesh):

time: 169 us -> 123 us (0.73)
  waiting for transfers between devices: 35.6 us -> 0 us
  Pallas kernels: 95.6 us -> 116 us
  blocking collectives: 20.2 us -> 0 us
  between operations: 13.4 us -> 0.02 us
    all_gather x1 -> x0, waiting for transfers between devices: 35.6 us -> none  [shards(): gathered = lax.all_gather(maps, 'tm', axis=0)]
    pallas_call x1, Pallas kernels: 7.79 us -> 28.2 us  [shards(): pl.pallas_call(functools.partial(return_kernel, streams, places, heads),...]
    all_to_all x1 -> x0, blocking collectives: 20.2 us -> none  [shards(): lax.all_to_all(mixed, 'stream', split_axis=0, concat_axis=1, tiled=True)]
    unnamed x1 -> x2, local copies, waits for them, and re-layouts: 0.12 us -> 2 us
  transfers between devices with their start and end apart: 1 -> 0, of which waited for: 1 -> 0; matrix products, arithmetic and copies ran while one was open for 0% -> 0% of each run, Pallas kernels for 0% -> 0%
where the time goes in v3:
time: 123 us; the launch traced here: 121 us
  Pallas kernels  116 us (94%)
  local copies, waits for them, and re-layouts  3.98 us (3%)
    pallas_call x1, Pallas kernels, shards(): pl.pallas_call(functools.partial(gather_kernel, streams, places, heads),...  59.6 us
    pallas_call x1, Pallas kernels, shards(): pl.pallas_call(functools.partial(return_kernel, streams, places, heads),...  28.2 us
    pallas_call x1, Pallas kernels, shards(): pl.pallas_call(functools.partial(block_kernel, heads), grid=(heads,), out...  28.1 us

profile of v3, /device:TPU:6, one launch (start us, length us, event | category | flops | bytes accessed | tf_op | source)
XLA Modules:
  0.0 120.8 jit_solution(16809213035335067642)
XLA Ops:
  0.0 1.3 %pad_bitcast_fusion = (f32[1,128]{1,0:T(1,128)}, f32[1,128]{1,0:T(1,128)}) fusion(f32[16]{0:T(128)} %param.16, f32[16]{0:T(128)} %param.15), kind=kLoop, calls=%fused_computation.1 | loop fusion | bytes 1152 | tf_op jit(solution)/shard_map/broadcast_in_dim | solution.py:555
  1.3 0.7 pad_maximum_fusion
  2.0 0.1 copy.11
  2.2 0.7 pad.12.clone
  2.8 59.6 %shard_map.91 = (bf16[4,128,2048]{2,1,0:T(8,128)(2,1)}, bf16[8,4,64,1664]{3,2,1,0:T(8,128)(2,1)}) custom-call(bf16[128,2048]{1,0:T(8,128)(2,1)} %tok_ref.1, bf16[8,64,2048]{2,1,0:T(8,128)(2,1)} %bitcast.11, bf16[8,64,2048]{2,1,0:T(8,128)(2,1)} %bitcast.12, bf16[8,64,2048]{2,1,0:T(8,128)(2,1)} %bitcast.13, bf16[8,64,128]{2,1,0:T(8,128)(2,1)} %bitcast.14), custom_call_target="tpu_custom_call" | custom-call | tf_op jit(solution)/shard_map/pallas_call | solution.py:526
  62.5 28.1 %shard_map.92 = (f32[512,512]{1,0:T(8,128)}, f32[512,512]{1,0:T(8,128)}, f32[4,256,128]{2,1,0:T(8,128)}) custom-call(bf16[512,2048]{1,0:T(8,128)(2,1)} %bitcast.10, bf16[8,4,64,1664]{3,2,1,0:T(8,128)(2,1)} %get-tuple-element.11.wq_ref.wk_ref.wv_ref.wg_ref, bf16[8,4,64,1664]{3,2,1,0:T(8,128)(2,1)} %get-tuple-element.11.wq_ref.wk_ref.wv_ref.wg_ref, ...), custom_call_target="tpu_custom_call" | custom-call | tf_op jit(solution)/shard_map/pallas_call | solution.py:558
  90.6 28.2 %shard_map.93 = bf16[128,2048]{1,0:T(8,128)(2,1)} custom-call(f32[512,512]{1,0:T(8,128)} %get-tuple-element.12.read_ref, f32[512,512]{1,0:T(8,128)} %get-tuple-element.13.query_ref, f32[4,256,128]{2,1,0:T(8,128)} %get-tuple-element.14.maps_ref, f32[1,128]{1,0:T(1,128)} %bitcast.15), custom_call_target="tpu_custom_call" | custom-call | tf_op jit(solution)/shard_map/pallas_call | solution.py:588
  118.9 1.9 %copy.13 = bf16[128,2048]{1,0:T(8,128)(2,1)} copy(bf16[128,2048]{1,0:T(8,128)(2,1)} %shard_map.93) | data formatting | bytes 1048576

commit v4 on v3

--- a/solution.py
+++ b/solution.py
@@ -28,9 +28,16 @@
 def dot3(a, b, ca, cb, batch=0):
     ah, al = halves(a)
     bh, bl = halves(b)
+    free = batch + (cb - batch + 1) % 2
     lead = tuple(range(batch))
-    dims = (((ca,), (cb,)), (lead, lead))
-    return contract(ah, bh, dims) + (contract(ah, bl, dims) + contract(al, bh, dims))
+    wide = jnp.concatenate([bh, bl], free)
+    both = contract(
+        jnp.concatenate([ah, al], ca),
+        jnp.concatenate([wide, wide], cb),
+        (((ca,), (cb,)), (lead, lead)),
+    )
+    half = both.shape[-1] // 2
+    return both[..., :half] + both[..., half:]
 
 
 def around(count):
@@ -233,10 +240,7 @@
 def block_kernel(
     heads,
     x_ref,
-    wq_ref,
-    wk_ref,
-    wv_ref,
-    wg_ref,
+    w_ref,
     rate_ref,
     bias_ref,
     read_ref,
@@ -247,15 +251,15 @@
     beta,
 ):
     first_head = lax.axis_index("stream") * heads
-    head = pl.program_id(0) + first_head
     rows = x_ref.shape[0]
-    places, streams, share, _ = wq_ref.shape
+    places, streams, share, _ = w_ref.shape
     depth = places * share
 
-    def project(refs):
+    def project(groups):
         total = None
         for s in range(streams):
-            w = jnp.concatenate([ref[:, s].reshape(depth, LANES) for ref in refs], 1)
+            parts = [w_ref[:, s, :, pl.ds(pl.multiple_of(at * LANES, LANES), LANES)] for at in groups]
+            w = jnp.concatenate([part.reshape(depth, LANES) for part in parts], 1)
             term = contract(x_ref[:, s * depth : (s + 1) * depth], w, (((1,), (0,)), ((), ())))
             total = term if total is None else total + term
         return total
@@ -264,37 +268,39 @@
     row_at = lax.broadcasted_iota(jnp.int32, (CHUNK, CHUNK), 0)
     col_at = lax.broadcasted_iota(jnp.int32, (CHUNK, CHUNK), 1)
 
-    @pl.when(pl.program_id(0) == 0)
-    def _():
-        logits = project((wg_ref,))
-        soft = jnp.maximum(logits, 0.0) + jnp.log1p(jnp.exp(-jnp.abs(logits)))
-        decay = (-rate_ref[...] * soft).astype(BF16)
-        beta[...] = (
-            (1.0 / (1.0 + jnp.exp(-(logits + bias_ref[...])))).astype(BF16).astype(F32)
-        ).reshape(chunks, CHUNK, LANES)
-        lower_ones = jnp.where(row_at >= col_at, 1.0, 0.0).astype(BF16)
-        for c in range(chunks):
-            piece = decay[c * CHUNK : (c + 1) * CHUNK]
-            sums = contract(lower_ones, piece, (((1,), (0,)), ((), ())))
-            cum[c] = sums
-            cum_row[c] = sums.T
-
-    raw = project((wq_ref, wk_ref, wv_ref))
-    raw_q = raw[:, :DK]
-    raw_k = raw[:, DK : 2 * DK]
-    q = (
-        raw_q * lax.rsqrt(jnp.sum(raw_q * raw_q, -1, keepdims=True) + 1e-06) * DK ** (-0.5)
-    ).astype(BF16)
-    k = (raw_k * lax.rsqrt(jnp.sum(raw_k * raw_k, -1, keepdims=True) + 1e-06)).astype(BF16)
-    v = raw[:, 2 * DK :].astype(BF16)
-    q = q.reshape(chunks, CHUNK, DK)
-    k = k.reshape(chunks, CHUNK, DK)
-    v = v.reshape(chunks, CHUNK, DV).astype(F32)
-
+    logits = project((3 * heads,))
+    soft = jnp.maximum(logits, 0.0) + jnp.log1p(jnp.exp(-jnp.abs(logits)))
+    decay = (-rate_ref[...] * soft).astype(BF16)
+    beta[...] = (
+        (1.0 / (1.0 + jnp.exp(-(logits + bias_ref[...])))).astype(BF16).astype(F32)
+    ).reshape(chunks, CHUNK, LANES)
+    lower_ones = jnp.where(row_at >= col_at, 1.0, 0.0).astype(BF16)
+    for c in range(chunks):
+        piece = decay[c * CHUNK : (c + 1) * CHUNK]
+        sums = contract(lower_ones, piece, (((1,), (0,)), ((), ())))
+        cum[c] = sums
+        cum_row[c] = sums.T
+
+    qs, ks, vs, gs, bs, g_rows = [], [], [], [], [], []
     lane = lax.broadcasted_iota(jnp.int32, (chunks, CHUNK, LANES), 2)
-    g = jnp.sum(jnp.where(lane == head, cum[...], 0.0), -1, keepdims=True)
-    b = jnp.sum(jnp.where(lane == head + HEADS, beta[...], 0.0), -1, keepdims=True)
-    g_row = cum_row[:, pl.ds(head, 1), :]
+    for h in range(heads):
+        raw = project([h + j * heads for j in range(3)])
+        raw_q = raw[:, :DK]
+        raw_k = raw[:, DK : 2 * DK]
+        q = (
+            raw_q * lax.rsqrt(jnp.sum(raw_q * raw_q, -1, keepdims=True) + 1e-06) * DK ** (-0.5)
+        ).astype(BF16)
+        k = (raw_k * lax.rsqrt(jnp.sum(raw_k * raw_k, -1, keepdims=True) + 1e-06)).astype(BF16)
+        v = raw[:, 2 * DK :].astype(BF16)
+        qs.append(q.reshape(chunks, CHUNK, DK))
+        ks.append(k.reshape(chunks, CHUNK, DK))
+        vs.append(v.reshape(chunks, CHUNK, DV))
+        head = first_head + h
+        gs.append(jnp.sum(jnp.where(lane == head, cum[...], 0.0), -1, keepdims=True))
+        bs.append(jnp.sum(jnp.where(lane == head + HEADS, beta[...], 0.0), -1, keepdims=True))
+        g_rows.append(cum_row[:, pl.ds(head, 1), :])
+    q, k, v, g, b, g_row = (jnp.concatenate(a, 0) for a in (qs, ks, vs, gs, bs, g_rows))
+    v = v.astype(F32)
     g_last = g[:, CHUNK - 1 :, :]
     growth = jnp.exp(g)
     tail = jnp.exp(g_last - g)
@@ -328,17 +334,24 @@
     jumps = dot3(jnp.swapaxes(wu, 1, 2), key_tail, 2, 1, 1)
     step_map = whole * eye[None] - jumps[:, :DK]
 
-    carry = jnp.concatenate([step_map[0], jumps[0, DK:]], 0)
-    query_ref[:CHUNK] = moved[0]
-    read_ref[:CHUNK] = mwu[0, :, DK:]
-    for c in range(1, chunks):
-        both = dot3(moved[c], carry, 1, 1)
+    carries = [None] * heads
+    for c in range(chunks):
         at = slice(c * CHUNK, (c + 1) * CHUNK)
-        query_ref[at] = both[:, :DK]
-        read_ref[at] = mwu[c, :, DK:] + both[:, DK:]
-        carry = dot3(carry, step_map[c], 1, 0)
-        carry = jnp.concatenate([carry[:DK], carry[DK:] + jumps[c, DK:]], 0)
-    state_ref[0] = carry
+        for h in range(heads):
+            n = h * chunks + c
+            lanes = slice(h * DK, (h + 1) * DK)
+            if c == 0:
+                query_ref[at, lanes] = moved[n]
+                read_ref[at, lanes] = mwu[n, :, DK:]
+                carries[h] = jnp.concatenate([step_map[n], jumps[n, DK:]], 0)
+                continue
+            both = dot3(moved[n], carries[h], 1, 1)
+            query_ref[at, lanes] = both[:, :DK]
+            read_ref[at, lanes] = mwu[n, :, DK:] + both[:, DK:]
+            carry = dot3(carries[h], step_map[n], 1, 0)
+            carries[h] = jnp.concatenate([carry[:DK], carry[DK:] + jumps[n, DK:]], 0)
+    for h in range(heads):
+        state_ref[h] = carries[h]
 
 
 def return_kernel(
@@ -557,32 +570,19 @@
     chunks = rows // CHUNK
     read, moved, maps = pl.pallas_call(
         functools.partial(block_kernel, heads),
-        grid=(heads,),
         out_shape=(
             jax.ShapeDtypeStruct((rows, heads * DV), F32),
             jax.ShapeDtypeStruct((rows, heads * DK), F32),
             jax.ShapeDtypeStruct((heads, DK + DV, DK), F32),
         ),
-        in_specs=[
-            pl.BlockSpec((rows, features), lambda h: (0, 0)),
-            pl.BlockSpec(full.shape[:3] + (DK,), lambda h: (0, 0, 0, h)),
-            pl.BlockSpec(full.shape[:3] + (DK,), lambda h: (0, 0, 0, heads + h)),
-            pl.BlockSpec(full.shape[:3] + (DV,), lambda h: (0, 0, 0, 2 * heads + h)),
-            pl.BlockSpec(full.shape[:3] + (LANES,), lambda h: (0, 0, 0, 3 * heads)),
-            pl.BlockSpec((1, LANES), lambda h: (0, 0)),
-            pl.BlockSpec((1, LANES), lambda h: (0, 0)),
-        ],
-        out_specs=(
-            pl.BlockSpec((rows, DV), lambda h: (0, h)),
-            pl.BlockSpec((rows, DK), lambda h: (0, h)),
-            pl.BlockSpec((1, DK + DV, DK), lambda h: (h, 0, 0)),
-        ),
+        in_specs=[pl.BlockSpec(memory_space=pltpu.VMEM)] * 4,
+        out_specs=(pl.BlockSpec(memory_space=pltpu.VMEM),) * 3,
         scratch_shapes=[
             pltpu.VMEM((chunks, CHUNK, LANES), F32),
             pltpu.VMEM((chunks, LANES, CHUNK), F32),
             pltpu.VMEM((chunks, CHUNK, LANES), F32),
         ],
-    )(x, full, full, full, full, rate, bias)
+    )(x, full, rate, bias)
 
     vmem = pl.BlockSpec(memory_space=pltpu.VMEM)
     return pl.pallas_call(

time: 123 us -> 113 us (0.919)
  Pallas kernels: 116 us -> 107 us
    pallas_call x1, Pallas kernels: 28.1 us -> 19 us  [shards(): pl.pallas_call(functools.partial(block_kernel, heads), out_shape=(jax.Sha...]
where the time goes in v4:
time: 113 us; the launch traced here: 111 us
  Pallas kernels  107 us (95%)
  local copies, waits for them, and re-layouts  3.98 us (4%)
    pallas_call x1, Pallas kernels, shards(): pl.pallas_call(functools.partial(gather_kernel, streams, places, heads),...  59.6 us
    pallas_call x1, Pallas kernels, shards(): pl.pallas_call(functools.partial(return_kernel, streams, places, heads),...  28.1 us
    pallas_call x1, Pallas kernels, shards(): pl.pallas_call(functools.partial(block_kernel, heads), out_shape=(jax.Sha...  19 us

profile of v4, /device:TPU:6, one launch (start us, length us, event | category | flops | bytes accessed | tf_op | source)
XLA Modules:
  0.0 111.5 jit_solution(6841140299947538880)
XLA Ops:
  0.0 1.3 %pad_bitcast_fusion = (f32[1,128]{1,0:T(1,128)}, f32[1,128]{1,0:T(1,128)}) fusion(f32[16]{0:T(128)} %param.16, f32[16]{0:T(128)} %param.15), kind=kLoop, calls=%fused_computation.1 | loop fusion | bytes 1152 | tf_op jit(solution)/shard_map/broadcast_in_dim | solution.py:568
  1.3 0.7 pad_maximum_fusion
  2.0 0.1 copy.11
  2.2 0.7 pad.12.clone
  2.8 59.6 %shard_map.91 = (bf16[4,128,2048]{2,1,0:T(8,128)(2,1)}, bf16[8,4,64,1664]{3,2,1,0:T(8,128)(2,1)}) custom-call(bf16[128,2048]{1,0:T(8,128)(2,1)} %tok_ref.1, bf16[8,64,2048]{2,1,0:T(8,128)(2,1)} %bitcast.11, bf16[8,64,2048]{2,1,0:T(8,128)(2,1)} %bitcast.12, bf16[8,64,2048]{2,1,0:T(8,128)(2,1)} %bitcast.13, bf16[8,64,128]{2,1,0:T(8,128)(2,1)} %bitcast.14), custom_call_target="tpu_custom_call" | custom-call | tf_op jit(solution)/shard_map/pallas_call | solution.py:539
  62.5 19.0 %shard_map.92 = (f32[512,512]{1,0:T(8,128)}, f32[512,512]{1,0:T(8,128)}, f32[4,256,128]{2,1,0:T(8,128)}) custom-call(bf16[512,2048]{1,0:T(8,128)(2,1)} %bitcast.10, bf16[8,4,64,1664]{3,2,1,0:T(8,128)(2,1)} %get-tuple-element.11.w_ref, f32[1,128]{1,0:T(1,128)} %get-tuple-element.16.rate_ref, f32[1,128]{1,0:T(1,128)} %get-tuple-element.15.bias_ref), custom_call_target="tpu_custom_call" | custom-call | tf_op jit(solution)/shard_map/pallas_call | solution.py:571
  81.5 28.1 %shard_map.93 = bf16[128,2048]{1,0:T(8,128)(2,1)} custom-call(f32[512,512]{1,0:T(8,128)} %get-tuple-element.12.read_ref, f32[512,512]{1,0:T(8,128)} %get-tuple-element.13.query_ref, f32[4,256,128]{2,1,0:T(8,128)} %get-tuple-element.14.maps_ref, f32[1,128]{1,0:T(1,128)} %bitcast.15), custom_call_target="tpu_custom_call" | custom-call | tf_op jit(solution)/shard_map/pallas_call | solution.py:588
  109.6 1.9 %copy.13 = bf16[128,2048]{1,0:T(8,128)(2,1)} copy(bf16[128,2048]{1,0:T(8,128)(2,1)} %shard_map.93) | data formatting | bytes 1048576
